TPU v7x, 256 devices: a whole 4x4x8 slice. The times are simulated.
256 devices in a mesh: ckpt: 8 (over z_hi, x), train: 32 (over y, z_lo, core).
Axes of the slice: x: 4, y: 4, z: 8 (z_hi: 2, z_lo: 4; z = z_hi * 4 + z_lo), core: 2. Of those that a mesh axis runs over, the one named last changes fastest.
Arguments:
- train_feat: bfloat16 [8, 65536, 1024], P('ckpt', 'train'), may hold values from -6 to 6
- test_feat: bfloat16 [8, 1024, 1024], P('ckpt', 'train'), may hold values from -0.375 to 0.375
- kernel_inv: bfloat16 [8, 1024, 1024], P('ckpt', 'train'), may hold values from -0.1875 to 0.1875
- bucket_weight: float32 [8, 16], P('ckpt'), may hold values from 0.2 to 2
- bucket: int32 [65536], P('train'), may hold values from 0 to 15
- test_order: int32 [1024], replicated, may hold values from 0 to 1023, each once
Outputs:
- scores: float32 [65536, 1024], P('train', 'ckpt')
Inputs may be any that keep to these rules, and one draw needn't show every extreme that they name: `test_order`: each of 0 to 1023 once.
All inputs are finite; a program needn't handle non-finite values.
Results may differ from a plain program's by a relative error of at most 0.012.
Values may be sent and summed in bfloat16 or wider, within the bound.
A program may use at most 64 MiB of HBM per device.

v0:
```python
import jax
import jax.numpy as jnp
from jax import lax
from jax.sharding import Mesh
from jax.sharding import PartitionSpec as P

TRAIN = ("train_0", "train_1", "train_2")
CKPT = ("ckpt_0", "ckpt_1")


def sent_to_all(shard, axis):
    size = lax.axis_size(axis)
    return lax.all_to_all(
        jnp.broadcast_to(shard[None], (size, *shard.shape)), axis, 0, 0, tiled=True
    )


def laid_out(blocks, dim):
    lengths = list(blocks.shape[1:])
    lengths[dim] *= blocks.shape[0]
    return jnp.moveaxis(blocks, 0, dim).reshape(lengths)


def gathered_by_axis(shard, axes, dim):
    far, near = axes
    blocks = sent_to_all(sent_to_all(shard, far), near)
    return laid_out(blocks.swapaxes(0, 1).reshape(-1, *shard.shape), dim)


def sum_in_order(blocks, axes, turns):
    lengths = [lax.axis_size(a) for a in axes]
    blocks = blocks.reshape(*lengths, *blocks.shape[1:])
    blocks = blocks.transpose(*turns, *range(len(axes), blocks.ndim))
    blocks = blocks.reshape(-1, *blocks.shape[len(axes) :])
    for k in turns:
        blocks = lax.psum_scatter(blocks, axes[k], scatter_dimension=0, tiled=True)
    return blocks[0]


def split_up(shard, dim, size):
    lengths = shard.shape
    blocks = shard.reshape(*lengths[:dim], size, lengths[dim] // size, *lengths[dim + 1 :])
    return jnp.moveaxis(blocks, dim, 0)


def summed_rows(shard, axes, turns, dim):
    size = lax.axis_size(axes)
    return sum_in_order(split_up(shard, dim, size), axes, turns)


def shards(train_feat, test_feat, kernel_inv, bucket_weight, bucket, test_order):
    local_ck = train_feat.shape[0]
    full_inverse = gathered_by_axis(kernel_inv, (("train_0", "train_1"), "train_2"), 1)
    local_rows = jnp.einsum(
        "kjb,kab->kja", test_feat, full_inverse, preferred_element_type=jnp.float32
    ).astype(jnp.bfloat16)
    stored = gathered_by_axis(local_rows, (("train_0", "train_1"), "train_2"), 1)
    ordered = jnp.zeros_like(stored).at[:, test_order, :].set(stored)
    onehot = (
        bucket[:, None] == jnp.arange(bucket_weight.shape[1], dtype=jnp.int32)[None, :]
    ).astype(jnp.float32)
    weights = jnp.dot(onehot, bucket_weight.T, precision=lax.Precision.HIGHEST)
    total = weights * jnp.dot(train_feat[0], ordered[0].T, preferred_element_type=jnp.float32)
    ensemble = local_ck * lax.axis_size(CKPT)
    summed = summed_rows(total.astype(jnp.bfloat16), CKPT, (1, 0), 1).astype(jnp.float32)
    return summed / ensemble


def solution(mesh):
    finer = Mesh(
        mesh.devices.reshape(2, 4, 4, 4, 2), ("ckpt_0", "ckpt_1", "train_0", "train_1", "train_2")
    )
    placed = (
        P(CKPT, TRAIN, None),
        P(CKPT, TRAIN, None),
        P(CKPT, TRAIN, None),
        P(CKPT, None),
        P(TRAIN),
        P(),
    )
    return jax.shard_map(
        shards, mesh=finer, in_specs=placed, out_specs=P(TRAIN, CKPT), check_vma=False
    )
```

profile of v0, /device:TPU:1, one launch (start us, length us, event | category | flops | bytes accessed | tf_op | source)
XLA Modules:
  0.0 212.3 jit_solution(3421520476598016508)
XLA Ops:
  6.5 0.0 copy-start
  6.5 1.0 broadcast_in_dim.41
  7.5 36.0 %all_to_all.20 = bf16[16,1,32,1024]{3,2,1,0:T(8,128)(2,1)S(1)} all-to-all(bf16[16,1,32,1024]{3,2,1,0:T(8,128)(2,1)S(1)} %broadcast_in_dim.41), channel_id=1, replica_groups=mesh['ckpt_0'=2,'ckpt_1'=4,'train_0'=4,'train_1'=4,'train_2'=2] {'train_..., dimensions={0} | all-to-all | bytes 2097152 | tf_op jit(solution)/shard_map/all_to_all | solution.py:13
  43.5 0.3 broadcast_in_dim.43
  43.8 6.7 %all_to_all.21 = bf16[2,16,1,32,1024]{4,3,1,2,0:T(8,128)(2,1)S(1)} all-to-all(bf16[2,16,1,32,1024]{4,3,1,2,0:T(8,128)(2,1)S(1)} %broadcast_in_dim.43), channel_id=1, replica_groups=mesh['ckpt_0'=2,'ckpt_1'=4,'train_0'=4,'train_1'=4,'train_2'=2] {'train_2'}, dimensions={0} | all-to-all | bytes 4194304 | tf_op jit(solution)/shard_map/all_to_all | solution.py:13
  50.5 0.3 copy.11
  50.8 0.0 copy-done
  50.8 0.7 convolution_convert_fusion
  51.5 0.0 copy-start.1
  51.5 0.0 copy-start.2
  51.5 0.0 copy-start.3
  51.6 1.1 broadcast_in_dim.44
  52.7 3.7 %all-to-all-start.2 = ((bf16[16,1,32,1024]{3,2,1,0:T(8,128)(2,1)}), bf16[16,1,32,1024]{3,2,1,0:T(8,128)(2,1)S(1)}, u32[]{:S(2)}, u32[]{:S(2)}) async-start(bf16[16,1,32,1024]{3,2,1,0:T(8,128)(2,1)} %broadcast_in_dim.44), calls=%async_computation.2 | async-start | bytes 2097152 | tf_op jit(solution)/shard_map/all_to_all | solution.py:13
  56.3 0.0 reduce-scatter.3.cloned.1.call-start
  56.4 0.0 copy-done.1
  56.4 0.0 copy-done.2
  56.4 0.0 copy-done.3
  56.4 0.7 fusion.3
  57.1 26.4 %all-to-all-done.2 = bf16[16,1,32,1024]{3,2,1,0:T(8,128)(2,1)S(1)} async-done(((bf16[16,1,32,1024]{3,2,1,0:T(8,128)(2,1)}), bf16[16,1,32,1024]{3,2,1,0:T(8,128)(2,1)S(1)}, u32[]{:S(2)}, u32[]{:S(2)}) %all-to-all-start.2) | async-done | bytes 1048608 | tf_op jit(solution)/shard_map/all_to_all | solution.py:13
  83.5 0.3 broadcast_in_dim.46
  83.8 6.6 %all_to_all.22 = bf16[2,16,1,32,1024]{4,3,1,2,0:T(8,128)(2,1)S(1)} all-to-all(bf16[2,16,1,32,1024]{4,3,1,2,0:T(8,128)(2,1)S(1)} %broadcast_in_dim.46), channel_id=1, replica_groups=mesh['ckpt_0'=2,'ckpt_1'=4,'train_0'=4,'train_1'=4,'train_2'=2] {'train_2'}, dimensions={0} | all-to-all | bytes 4194304 | tf_op jit(solution)/shard_map/all_to_all | solution.py:13
  90.4 1.5 copy.12
  91.8 6.6 %scatter_custom_fusion = bf16[1024,1024]{1,0:T(8,128)(2,1)S(1)} fusion(s32[1024]{0:T(1024)S(1)} %compare_select_fusion, bf16[1024,1024]{1,0:T(8,128)(2,1)} %bitcast.40, bf16[]{:T(256)} %constant.1.clone.1), kind=kCustom, calls=%fused_computation.4 | custom fusion | bytes 2097664 | tf_op jit(solution)/shard_map/scatter | solution.py:58
  98.4 8.4 %multiply_convert_fusion = bf16[1024,2048]{1,0:T(8,128)(2,1)} fusion(bf16[1024,1024]{1,0:T(8,128)(2,1)S(1)} %scatter_custom_fusion, bf16[1,2048,1024]{2,1,0:T(8,128)(2,1)} %param.6, f32[2048]{0:T(1024)S(1)} %bitcast.42), kind=kOutput, calls=%fused_computation.1 | convolution fusion | flops 4299161600 | bytes 10493952 | tf_op jit(solution)/shard_map/dot_general | solution.py:63
  106.8 6.3 %copy.13 = bf16[2,4,2048,128]{3,2,0,1:T(8,128)(2,1)} copy(bf16[2,4,2048,128]{2,3,1,0:T(8,128)(2,1)} %bitcast.39) | data formatting | bytes 8388608 | tf_op jit(solution)/shard_map/reshape | solution.py:32
  113.1 0.0 reduce-scatter.3.cloned.1.call-update
  113.1 0.0 reduce-scatter.5.cloned.1.call-start
  113.2 47.0 %reduce-scatter.3.cloned.1.call-done = bf16[2,2048,128]{2,1,0:T(8,128)(2,1)} async-done(((bf16[8,2048,128]{2,1,0:T(8,128)(2,1)}), bf16[2,2048,128]{2,1,0:T(8,128)(2,1)}) %reduce-scatter.3.cloned.1.call-update) | async-done | bytes 1048592 | tf_op jit(solution)/shard_map/reduce_scatter | solution.py:36
  160.2 0.0 reduce-scatter.5.cloned.1.call-update
  160.2 43.2 %reduce-scatter.5.cloned.1.call-done = bf16[1,2048,128]{2,1,0:T(8,128)(2,1)} async-done(((bf16[2,2048,128]{2,1,0:T(8,128)(2,1)}), bf16[1,2048,128]{2,1,0:T(8,128)(2,1)}) %reduce-scatter.5.cloned.1.call-update) | async-done | bytes 524304 | tf_op jit(solution)/shard_map/reduce_scatter | solution.py:36
  203.4 2.1 multiply_bitcast_fusion
  (1 shorter events, 0.0 us)
Async XLA Ops:
  6.5 44.3 %copy-start = (bf16[1,32,1024]{2,1,0:T(8,128)(2,1)S(1)}, bf16[1,32,1024]{2,1,0:T(8,128)(2,1)}, u32[]{:S(2)}) copy-start(bf16[1,32,1024]{2,1,0:T(8,128)(2,1)} %param.7) | copy-start | bytes 196612
  51.5 4.9 %copy-start.1 = (s32[1024]{0:T(1024)S(1)}, s32[1024]{0:T(1024)}, u32[]{:S(2)}) copy-start(s32[1024]{0:T(1024)} %param.11) | copy-start | bytes 12292
  51.5 4.9 %copy-start.2 = (s32[2048]{0:T(1024)S(1)}, s32[2048]{0:T(1024)}, u32[]{:S(2)}) copy-start(s32[2048]{0:T(1024)} %param.10) | copy-start | bytes 24580
  51.5 4.9 %copy-start.3 = (f32[1,16]{1,0:T(1,128)S(1)}, f32[1,16]{1,0:T(1,128)}, u32[]{:S(2)}) copy-start(f32[1,16]{1,0:T(1,128)} %param.9) | copy-start | bytes 196
  52.7 30.8 %all-to-all-start.2 = ((bf16[16,1,32,1024]{3,2,1,0:T(8,128)(2,1)}), bf16[16,1,32,1024]{3,2,1,0:T(8,128)(2,1)S(1)}, u32[]{:S(2)}, u32[]{:S(2)}) async-start(bf16[16,1,32,1024]{3,2,1,0:T(8,128)(2,1)} %broadcast_in_dim.44), calls=%async_computation.2 | async-start | bytes 2097152 | tf_op jit(solution)/shard_map/all_to_all | solution.py:13
  56.3 103.9 %reduce-scatter.3.cloned.1.call-start = ((), (), s32[]{:S(2)}) async-start(), calls=%async_computation.6 | async-start | bytes 5242880 | tf_op jit(solution)/shard_map/reduce_scatter | solution.py:36
  113.1 90.3 %reduce-scatter.5.cloned.1.call-start = ((), (), s32[]{:S(2)}) async-start(), calls=%async_computation.7 | async-start | bytes 1572864 | tf_op jit(solution)/shard_map/reduce_scatter | solution.py:36
Sparse Core Ops, SparseCore 0:
  113.3 46.9 reduce-scatter.2
  162.7 40.6 reduce-scatter.4
where the time goes:
time: 213 us; the launch traced here: 212 us
  waiting for transfers between devices  117 us (55%)
  blocking collectives  49.3 us (23%)
  local copies, waits for them, and re-layouts  17.3 us (8%)
  between operations  13.5 us (6%)
  matrix products  9.83 us (5%)
  starting transfers between devices  3.74 us (2%)
    reduce_scatter x2, waiting for transfers between devices, sum_in_order(): blocks = lax.psum_scatter(blocks, axes[k], scatter_dimension=0, tiled=True)  90.2 us
    all_to_all x3, blocking collectives, sent_to_all(): lax.all_to_all(jnp.broadcast_to(shard[None], (size, *shard.shape)), axis,...  49.3 us
    all_to_all x1, waiting for transfers between devices, sent_to_all(): lax.all_to_all(jnp.broadcast_to(shard[None], (size, *shard.shape)), axis,...  26.4 us
    dot_general x1, matrix products, shards(): jnp.dot(train_feat[0], ordered[0].T, preferred_element_type=jnp.float32)  8.4 us
    scatter x1, local copies, waits for them, and re-layouts, shards(): ordered = jnp.zeros_like(stored).at[:, test_order, :].set(stored)  6.58 us
    reshape x1, local copies, waits for them, and re-layouts, sum_in_order(): blocks = blocks.reshape(*lengths, *blocks.shape[1:])  6.28 us
  transfers between devices with their start and end apart: 3, of which 3 were waited for; matrix products, arithmetic and copies ran while one was open for 0% of the time, Pallas kernels for 0%

commit v1 on v0

v1 whole, which is shorter than its diff:
```python
import functools

import jax
import jax.numpy as jnp
from jax import lax
from jax.experimental import pallas as pl
from jax.experimental.pallas import tpu as pltpu
from jax.sharding import PartitionSpec as P

MESH = pl.DeviceIdType.MESH
F32 = jnp.float32
BF16 = jnp.bfloat16
ROWS = 256
NT = (((1,), (1,)), ((), ()))
TN = (((0,), (0,)), ((), ()))


def kernel(
    train_hbm, test_hbm, kinv_hbm, bw_ref, bucket_ref, order_ref, out_ref,
    train, gb, tp, ob, wcol, s2, sp, sm, far_l, far_r, got_l, got_r, own, zs, zr,
    load_sem, g_send, g_recv, sib_send, sib_recv, s2_send, sp_send, sm_send,
    far_l_recv, far_r_recv, got_l_recv, got_r_recv, z_send, z_recv,
):
    ck = lax.axis_index("ckpt")
    tr = lax.axis_index("train")
    zh, x = ck // 4, ck % 4
    y, z, c = tr // 8, (tr // 2) % 4, tr % 2

    def at_train(yy, zz, cc):
        return {"ckpt": ck, "train": (yy * 4 + zz) * 2 + cc}

    def at_ckpt(zz, xx):
        return {"ckpt": zz * 4 + xx, "train": tr}

    fold = z // 2
    w = z + fold * (3 - 2 * z)

    def zplace(s):
        if s == 0:
            return z
        v = s - 1 + (s - 1 - w + 4) // 4
        return v + fold * (3 - 2 * v)

    y_up, y_dn, y_far = (y + 1) % 4, (y + 3) % 4, (y + 2) % 4
    up, dn = at_train(y_up, z, c), at_train(y_dn, z, c)
    sib = at_train(y, z, 1 - c)
    right, left = at_ckpt(zh, (x + 1) % 4), at_ckpt(zh, (x + 3) % 4)
    across = at_ckpt(1 - zh, x)

    loads = [
        pltpu.make_async_copy(test_hbm, gb.at[0, tr], load_sem.at[0]),
        pltpu.make_async_copy(kinv_hbm, gb.at[1, tr], load_sem.at[1]),
        pltpu.make_async_copy(train_hbm, train, load_sem.at[2]),
    ]
    for cp in loads:
        cp.start()

    barrier = pltpu.get_barrier_semaphore()
    partners = [up, dn, sib, right, left, across]
    partners += [at_train(y, zplace(s), c) for s in (1, 2, 3)]
    for d in partners:
        pl.semaphore_signal(barrier, inc=1, device_id=d, device_id_type=MESH)
    pl.semaphore_wait(barrier, len(partners))
    loads[0].wait()
    loads[1].wait()

    started = []
    counts = [0, 0]

    def g_copy(m, yy, zz, send, dev):
        chunk = (yy * 4 + zz) * 2 + c
        return pltpu.make_async_remote_copy(
            src_ref=gb.at[m, chunk], dst_ref=gb.at[m, chunk], send_sem=send,
            recv_sem=g_recv.at[m, yy, zz], device_id=dev, device_id_type=MESH,
        )

    def g_start(m, yy, zz, dev):
        cp = g_copy(m, yy, zz, g_send.at[m, counts[m]], dev)
        counts[m] += 1
        cp.start()
        started.append(cp)

    def g_wait(m, yy, zz):
        g_copy(m, yy, zz, g_send.at[m, 0], up).wait_recv()

    def sib_copy(m, yy, zz, cc):
        chunk = (yy * 4 + zz) * 2 + cc
        return pltpu.make_async_remote_copy(
            src_ref=gb.at[m, chunk], dst_ref=gb.at[m, chunk], send_sem=sib_send.at[m, yy, zz],
            recv_sem=sib_recv.at[m, yy, zz], device_id=sib, device_id_type=MESH,
        )

    def to_sib(m, yy, zz):
        cp = sib_copy(m, yy, zz, c)
        cp.start()
        started.append(cp)

    def begin(m):
        g_start(m, y, z, up)
        g_start(m, y, z, dn)
        for s in (1, 2, 3):
            g_start(m, y, z, at_train(y, zplace(s), c))
        to_sib(m, y, z)

    def from_line(m, s):
        zz = zplace(s)
        g_wait(m, y, zz)
        g_start(m, y, zz, up)
        g_start(m, y, zz, dn)
        to_sib(m, y, zz)

    def from_ring(m, s):
        zz = zplace(s)
        g_wait(m, y_dn, zz)
        if s % 2 == 0:
            g_start(m, y_dn, zz, up)
        to_sib(m, y_dn, zz)
        g_wait(m, y_up, zz)
        if s % 2 == 1:
            g_start(m, y_up, zz, dn)
        to_sib(m, y_up, zz)

    def from_far(m, s):
        zz = zplace(s)
        g_wait(m, y_far, zz)
        to_sib(m, y_far, zz)

    def from_sib(m):
        def step(i, carry):
            sib_copy(m, i // 4, i % 4, 1 - c).wait_recv()
            return carry
        lax.fori_loop(0, 16, step, 0)

    def blocks(h, p):
        side = zh if h == 1 else 1 - zh
        first, second = ((x + 2) % 4, x) if p == 0 else ((x + 1) % 4, (x + 3) % 4)
        return (side * 4 + first) * 128, (side * 4 + second) * 128

    def permute(h, p):
        a, b = blocks(h, p)
        order = order_ref[...]
        j = lax.broadcasted_iota(jnp.int32, (128, 1), 0)
        pick = jnp.concatenate(
            [(order == j + a).astype(F32).astype(BF16), (order == j + b).astype(F32).astype(BF16)], axis=0
        )

        def step(i, carry):
            cols = pl.ds(pl.multiple_of(i * 256, 256), 256)
            rows = gb[0, :, :, cols].reshape(1024, 256)
            tp[2 * h + p, :, cols] = jnp.dot(pick, rows, preferred_element_type=F32).astype(BF16)
            return carry
        lax.fori_loop(0, 4, step, 0)

    def transform(h, p):
        def step(i, carry):
            inv = gb[1, pl.ds(i * 8, 8)].reshape(256, 1024)
            cols = pl.ds(pl.multiple_of(i * 256, 256), 256)
            ob[2 * h + p, :, cols] = lax.dot_general(
                tp[2 * h + p], inv, NT, preferred_element_type=F32
            ).astype(BF16)
            return carry
        lax.fori_loop(0, 4, step, 0)

    begin(0)
    begin(1)

    eye = lax.broadcasted_iota(jnp.int32, (16, 16), 0) == lax.broadcasted_iota(jnp.int32, (16, 16), 1)
    col = jnp.sum(jnp.where(eye, jnp.broadcast_to(bw_ref[...], (16, 16)), 0.0), axis=1, keepdims=True)
    col = jnp.broadcast_to(col, (16, 128))
    hi = col.astype(BF16)
    rest = col - hi.astype(F32)
    mid = rest.astype(BF16)
    low = (rest - mid.astype(F32)).astype(BF16)

    def weigh(i, carry):
        rows = pl.ds(pl.multiple_of(i * ROWS, ROWS), ROWS)
        b = bucket_ref[:, rows]
        hot = (lax.broadcasted_iota(jnp.int32, (16, 1), 0) == b).astype(F32).astype(BF16)
        acc = lax.dot_general(hot, hi, TN, preferred_element_type=F32)
        acc += lax.dot_general(hot, mid, TN, preferred_element_type=F32)
        acc += lax.dot_general(hot, low, TN, preferred_element_type=F32)
        wcol[i] = acc
        return carry
    lax.fori_loop(0, 8, weigh, 0)

    from_line(0, 1)
    from_ring(0, 0)
    from_line(0, 2)
    from_ring(0, 1)
    from_ring(1, 0)
    from_line(0, 3)
    from_ring(0, 2)
    from_line(1, 1)
    from_ring(0, 3)
    from_line(1, 2)
    from_ring(1, 1)
    for s in range(4):
        from_far(0, s)
    from_line(1, 3)
    from_sib(0)
    permute(0, 0)
    from_ring(1, 2)
    permute(0, 1)
    from_ring(1, 3)
    permute(1, 0)
    from_far(1, 0)
    from_far(1, 1)
    from_far(1, 2)
    permute(1, 1)
    from_far(1, 3)
    loads[2].wait()
    from_sib(1)

    def tile(r, k):
        rows = pl.ds(pl.multiple_of(r * ROWS, ROWS), ROWS)
        t = lax.dot_general(train[rows, :], ob[k], NT, preferred_element_type=F32)
        return t[:, :128] * wcol[r], t[:, 128:] * wcol[r]

    def far_copy(h, i, r, to_right):
        return pltpu.make_async_remote_copy(
            src_ref=s2.at[h, r], dst_ref=(far_l if to_right else far_r).at[h, i], send_sem=s2_send.at[h, r],
            recv_sem=(far_l_recv if to_right else far_r_recv).at[h, i],
            device_id=right if to_right else left, device_id_type=MESH,
        )

    def right_copy(h, r):
        return pltpu.make_async_remote_copy(
            src_ref=sp.at[h, r], dst_ref=got_l.at[h, r], send_sem=sp_send.at[h, r],
            recv_sem=got_l_recv.at[h, r], device_id=right, device_id_type=MESH,
        )

    def left_copy(h, r):
        return pltpu.make_async_remote_copy(
            src_ref=sm.at[h, r], dst_ref=got_r.at[h, r], send_sem=sm_send.at[h, r],
            recv_sem=got_r_recv.at[h, r], device_id=left, device_id_type=MESH,
        )

    def z_copy(r):
        return pltpu.make_async_remote_copy(
            src_ref=zs.at[r], dst_ref=zr.at[r], send_sem=z_send.at[r],
            recv_sem=z_recv.at[r], device_id=across, device_id_type=MESH,
        )

    def far_blocks(h):
        def step(i, carry):
            for half in (0, 1):
                r = i + 4 * half
                a, b = tile(r, 2 * h)
                s2[h, r] = a.astype(BF16)
                own[h, r] = b
                far_copy(h, i, r, half == 0).start()
            return carry
        lax.fori_loop(0, 4, step, 0)

    def near_blocks(h):
        def step(i, carry):
            p, m = tile(i, 2 * h + 1)
            sm[h, i] = m.astype(BF16)
            left_copy(h, i).start()
            far_copy(h, i, i, True).wait_recv()
            sp[h, i] = (p + far_l[h, i].astype(F32)).astype(BF16)
            right_copy(h, i).start()
            r = i + 4
            p, m = tile(r, 2 * h + 1)
            sp[h, r] = p.astype(BF16)
            right_copy(h, r).start()
            far_copy(h, i, r, False).wait_recv()
            sm[h, r] = (m + far_r[h, i].astype(F32)).astype(BF16)
            left_copy(h, r).start()
            return carry
        lax.fori_loop(0, 4, step, 0)

    def add_up(h):
        def step(i, carry):
            for half in (0, 1):
                r = i + 4 * half
                right_copy(h, r).wait_recv()
                left_copy(h, r).wait_recv()
                v = own[h, r] + got_l[h, r].astype(F32) + got_r[h, r].astype(F32)
                if h == 0:
                    zs[r] = v.astype(BF16)
                    z_copy(r).start()
                else:
                    own[h, r] = v
            return carry
        lax.fori_loop(0, 4, step, 0)

    transform(0, 0)
    far_blocks(0)
    transform(0, 1)
    near_blocks(0)
    transform(1, 0)
    far_blocks(1)
    transform(1, 1)
    add_up(0)
    near_blocks(1)
    add_up(1)

    def finish(i, carry):
        for half in (0, 1):
            r = i + 4 * half
            z_copy(r).wait_recv()
            rows = pl.ds(pl.multiple_of(r * ROWS, ROWS), ROWS)
            out_ref[rows, :] = (own[1, r] + zr[r].astype(F32)) * 0.125
        return carry
    lax.fori_loop(0, 4, finish, 0)

    for cp in started:
        cp.wait_send()

    def drain(r, carry):
        for h in (0, 1):
            far_copy(h, 0, r, True).wait_send()
            right_copy(h, r).wait_send()
            left_copy(h, r).wait_send()
        z_copy(r).wait_send()
        return carry
    lax.fori_loop(0, 8, drain, 0)


def shards(train_feat, test_feat, kernel_inv, bucket_weight, bucket, test_order):
    anywhere = pl.BlockSpec(memory_space=pl.ANY)
    vmem = pl.BlockSpec(memory_space=pltpu.VMEM)
    dma = pltpu.SemaphoreType.DMA
    return pl.pallas_call(
        kernel,
        out_shape=jax.ShapeDtypeStruct((2048, 128), F32),
        in_specs=[anywhere, anywhere, anywhere, vmem, vmem, vmem],
        out_specs=vmem,
        scratch_shapes=[
            pltpu.VMEM((2048, 1024), BF16),
            pltpu.VMEM((2, 32, 32, 1024), BF16),
            pltpu.VMEM((4, 256, 1024), BF16),
            pltpu.VMEM((4, 256, 1024), BF16),
            pltpu.VMEM((8, ROWS, 128), F32),
            pltpu.VMEM((2, 8, ROWS, 128), BF16),
            pltpu.VMEM((2, 8, ROWS, 128), BF16),
            pltpu.VMEM((2, 8, ROWS, 128), BF16),
            pltpu.VMEM((2, 4, ROWS, 128), BF16),
            pltpu.VMEM((2, 4, ROWS, 128), BF16),
            pltpu.VMEM((2, 8, ROWS, 128), BF16),
            pltpu.VMEM((2, 8, ROWS, 128), BF16),
            pltpu.VMEM((2, 8, ROWS, 128), F32),
            pltpu.VMEM((8, ROWS, 128), BF16),
            pltpu.VMEM((8, ROWS, 128), BF16),
            dma((3,)),
            dma((2, 16)),
            dma((2, 4, 4)),
            dma((2, 4, 4)),
            dma((2, 4, 4)),
            dma((2, 8)),
            dma((2, 8)),
            dma((2, 8)),
            dma((2, 4)),
            dma((2, 4)),
            dma((2, 8)),
            dma((2, 8)),
            dma((8,)),
            dma((8,)),
        ],
        compiler_params=pltpu.CompilerParams(
            collective_id=0, has_side_effects=True, vmem_limit_bytes=60 * 1024 * 1024
        ),
        name="scores",
    )(
        train_feat[0], test_feat[0], kernel_inv[0], bucket_weight,
        bucket.reshape(1, 2048), test_order.reshape(1, 1024),
    )


def solution(mesh):
    return jax.shard_map(
        shards, mesh=mesh,
        in_specs=(P("ckpt", "train", None), P("ckpt", "train", None), P("ckpt", "train", None),
                  P("ckpt", None), P("train"), P(None)),
        out_specs=P("train", "ckpt"), check_vma=False,
    )
```

time: 213 us -> 87.4 us (0.41)
  waiting for transfers between devices: 117 us -> 0 us
  Pallas kernels: 0 us -> 85 us
  blocking collectives: 49.3 us -> 0 us
  local copies, waits for them, and re-layouts: 17.3 us -> 2.26 us
  between operations: 13.5 us -> 0.01 us
  matrix products: 9.83 us -> 0 us
  starting transfers between devices: 3.74 us -> 0 us
    reduce_scatter x2 -> x0, waiting for transfers between devices: 90.2 us -> none  [sum_in_order(): blocks = lax.psum_scatter(blocks, axes[k], scatter_dimension=0, tiled=True)]
    pallas_call x0 -> x1, Pallas kernels: none -> 85 us  [shards(): pl.pallas_call(kernel, out_shape=jax.ShapeDtypeStruct((2048, 128), F32),...]
    all_to_all x3 -> x0, blocking collectives: 49.3 us -> none  [sent_to_all(): lax.all_to_all(jnp.broadcast_to(shard[None], (size, *shard.shape)), axis,...]
    all_to_all x1 -> x0, waiting for transfers between devices: 26.4 us -> none  [sent_to_all(): lax.all_to_all(jnp.broadcast_to(shard[None], (size, *shard.shape)), axis,...]
    dot_general x3 -> x0, matrix products: 9.83 us -> none  [the longest x1 8.4 us: shards(): jnp.dot(train_feat[0], ordered[0].T, preferred_element_type=jnp.float32)]
    scatter x1 -> x0, local copies, waits for them, and re-layouts: 6.58 us -> none  [shards(): ordered = jnp.zeros_like(stored).at[:, test_order, :].set(stored)]
    reshape x1 -> x0, local copies, waits for them, and re-layouts: 6.28 us -> none  [sum_in_order(): blocks = blocks.reshape(*lengths, *blocks.shape[1:])]
    all_to_all x1 -> x0, starting transfers between devices: 3.66 us -> none  [sent_to_all(): lax.all_to_all(jnp.broadcast_to(shard[None], (size, *shard.shape)), axis,...]
  transfers between devices with their start and end apart: 3 -> 0, of which waited for: 3 -> 0; matrix products, arithmetic and copies ran while one was open for 0% -> 0% of each run, Pallas kernels for 0% -> 0%
where the time goes in v1:
time: 87.4 us; the launch traced here: 87.3 us
  Pallas kernels  85 us (97%)
  local copies, waits for them, and re-layouts  2.26 us (3%)
    pallas_call x1, Pallas kernels, shards(): pl.pallas_call(kernel, out_shape=jax.ShapeDtypeStruct((2048, 128), F32),...  85 us
    unnamed x1, local copies, waits for them, and re-layouts  2.26 us

profile of v1, /device:TPU:1, one launch (start us, length us, event | category | flops | bytes accessed | tf_op | source)
XLA Modules:
  0.0 87.3 jit_solution(12718210795814506873)
XLA Ops:
  0.0 85.0 %scores.1 = f32[2048,128]{1,0:T(8,128)} custom-call(bf16[2048,1024]{1,0:T(8,128)(2,1)} %bitcast.5, bf16[32,1024]{1,0:T(8,128)(2,1)} %bitcast.6, bf16[32,1024]{1,0:T(8,128)(2,1)} %bitcast.7, f32[1,16]{1,0:T(1,128)} %bw_ref.1, s32[1,2048]{1,0:T(1,128)} %bitcast.8, s32[1,1024]{1,0:T(1,128)} %bitcast.9), custom_call_target="tpu_custom_call" | custom-call | tf_op jit(solution)/shard_map/scores/pallas_call | solution.py:325
  85.0 2.3 %copy.8 = f32[2048,128]{1,0:T(8,128)} copy(f32[2048,128]{1,0:T(8,128)} %scores.1) | data formatting | bytes 2097152

commit v2 on v1

--- a/solution.py
+++ b/solution.py
@@ -17,8 +17,8 @@
 
 def kernel(
     train_hbm, test_hbm, kinv_hbm, bw_ref, bucket_ref, order_ref, out_ref,
-    train, gb, tp, ob, wcol, s2, sp, sm, far_l, far_r, got_l, got_r, own, zs, zr,
-    load_sem, g_send, g_recv, sib_send, sib_recv, s2_send, sp_send, sm_send,
+    train, tb, kb, gb, ob, wcol, s2, sp, sm, far_l, far_r, got_l, got_r, own, zs, zr,
+    load_sem, t_send, t_recv, k_send, k_recv, k_sib, b_send, b_recv, b_sib, s2_send, sp_send, sm_send,
     far_l_recv, far_r_recv, got_l_recv, got_r_recv, z_send, z_recv,
 ):
     ck = lax.axis_index("ckpt")
@@ -48,121 +48,43 @@
     across = at_ckpt(1 - zh, x)
 
     loads = [
-        pltpu.make_async_copy(test_hbm, gb.at[0, tr], load_sem.at[0]),
-        pltpu.make_async_copy(kinv_hbm, gb.at[1, tr], load_sem.at[1]),
+        pltpu.make_async_copy(test_hbm, tb.at[y], load_sem.at[0]),
+        pltpu.make_async_copy(kinv_hbm, kb.at[z, c], load_sem.at[1]),
         pltpu.make_async_copy(train_hbm, train, load_sem.at[2]),
     ]
     for cp in loads:
         cp.start()
 
     barrier = pltpu.get_barrier_semaphore()
-    partners = [up, dn, sib, right, left, across]
+    partners = [up, dn, at_train(y_far, z, c), sib, right, left, across]
     partners += [at_train(y, zplace(s), c) for s in (1, 2, 3)]
     for d in partners:
         pl.semaphore_signal(barrier, inc=1, device_id=d, device_id_type=MESH)
     pl.semaphore_wait(barrier, len(partners))
-    loads[0].wait()
-    loads[1].wait()
 
     started = []
-    counts = [0, 0]
-
-    def g_copy(m, yy, zz, send, dev):
-        chunk = (yy * 4 + zz) * 2 + c
-        return pltpu.make_async_remote_copy(
-            src_ref=gb.at[m, chunk], dst_ref=gb.at[m, chunk], send_sem=send,
-            recv_sem=g_recv.at[m, yy, zz], device_id=dev, device_id_type=MESH,
-        )
-
-    def g_start(m, yy, zz, dev):
-        cp = g_copy(m, yy, zz, g_send.at[m, counts[m]], dev)
-        counts[m] += 1
+
+    def send(ref, send_sem, recv_sem, dev):
+        cp = pltpu.make_async_remote_copy(
+            src_ref=ref, dst_ref=ref, send_sem=send_sem, recv_sem=recv_sem, device_id=dev, device_id_type=MESH,
+        )
         cp.start()
         started.append(cp)
 
-    def g_wait(m, yy, zz):
-        g_copy(m, yy, zz, g_send.at[m, 0], up).wait_recv()
-
-    def sib_copy(m, yy, zz, cc):
-        chunk = (yy * 4 + zz) * 2 + cc
-        return pltpu.make_async_remote_copy(
-            src_ref=gb.at[m, chunk], dst_ref=gb.at[m, chunk], send_sem=sib_send.at[m, yy, zz],
-            recv_sem=sib_recv.at[m, yy, zz], device_id=sib, device_id_type=MESH,
-        )
-
-    def to_sib(m, yy, zz):
-        cp = sib_copy(m, yy, zz, c)
-        cp.start()
-        started.append(cp)
-
-    def begin(m):
-        g_start(m, y, z, up)
-        g_start(m, y, z, dn)
-        for s in (1, 2, 3):
-            g_start(m, y, z, at_train(y, zplace(s), c))
-        to_sib(m, y, z)
-
-    def from_line(m, s):
-        zz = zplace(s)
-        g_wait(m, y, zz)
-        g_start(m, y, zz, up)
-        g_start(m, y, zz, dn)
-        to_sib(m, y, zz)
-
-    def from_ring(m, s):
-        zz = zplace(s)
-        g_wait(m, y_dn, zz)
-        if s % 2 == 0:
-            g_start(m, y_dn, zz, up)
-        to_sib(m, y_dn, zz)
-        g_wait(m, y_up, zz)
-        if s % 2 == 1:
-            g_start(m, y_up, zz, dn)
-        to_sib(m, y_up, zz)
-
-    def from_far(m, s):
-        zz = zplace(s)
-        g_wait(m, y_far, zz)
-        to_sib(m, y_far, zz)
-
-    def from_sib(m):
-        def step(i, carry):
-            sib_copy(m, i // 4, i % 4, 1 - c).wait_recv()
-            return carry
-        lax.fori_loop(0, 16, step, 0)
-
-    def blocks(h, p):
-        side = zh if h == 1 else 1 - zh
-        first, second = ((x + 2) % 4, x) if p == 0 else ((x + 1) % 4, (x + 3) % 4)
-        return (side * 4 + first) * 128, (side * 4 + second) * 128
-
-    def permute(h, p):
-        a, b = blocks(h, p)
-        order = order_ref[...]
-        j = lax.broadcasted_iota(jnp.int32, (128, 1), 0)
-        pick = jnp.concatenate(
-            [(order == j + a).astype(F32).astype(BF16), (order == j + b).astype(F32).astype(BF16)], axis=0
-        )
-
-        def step(i, carry):
-            cols = pl.ds(pl.multiple_of(i * 256, 256), 256)
-            rows = gb[0, :, :, cols].reshape(1024, 256)
-            tp[2 * h + p, :, cols] = jnp.dot(pick, rows, preferred_element_type=F32).astype(BF16)
-            return carry
-        lax.fori_loop(0, 4, step, 0)
-
-    def transform(h, p):
-        def step(i, carry):
-            inv = gb[1, pl.ds(i * 8, 8)].reshape(256, 1024)
-            cols = pl.ds(pl.multiple_of(i * 256, 256), 256)
-            ob[2 * h + p, :, cols] = lax.dot_general(
-                tp[2 * h + p], inv, NT, preferred_element_type=F32
-            ).astype(BF16)
-            return carry
-        lax.fori_loop(0, 4, step, 0)
-
-    begin(0)
-    begin(1)
+    def arrived(ref, recv_sem):
+        pltpu.make_async_remote_copy(
+            src_ref=ref, dst_ref=ref, send_sem=b_send.at[0], recv_sem=recv_sem, device_id=sib, device_id_type=MESH,
+        ).wait_recv()
+
+    ring = [at_train(y_far, z, c), up, dn]
+
+    loads[1].wait()
+    for s in (1, 2, 3):
+        send(kb.at[z, c], k_send.at[s], k_recv.at[z], at_train(y, zplace(s), c))
+    send(kb.at[z, c], k_send.at[0], k_sib.at[z], sib)
+    loads[0].wait()
+    for i, d in enumerate(ring):
+        send(tb.at[y], t_send.at[i], t_recv.at[y], d)
 
     eye = lax.broadcasted_iota(jnp.int32, (16, 16), 0) == lax.broadcasted_iota(jnp.int32, (16, 16), 1)
     col = jnp.sum(jnp.where(eye, jnp.broadcast_to(bw_ref[...], (16, 16)), 0.0), axis=1, keepdims=True)
@@ -183,33 +105,69 @@
         return carry
     lax.fori_loop(0, 8, weigh, 0)
 
-    from_line(0, 1)
-    from_ring(0, 0)
-    from_line(0, 2)
-    from_ring(0, 1)
-    from_ring(1, 0)
-    from_line(0, 3)
-    from_ring(0, 2)
-    from_line(1, 1)
-    from_ring(0, 3)
-    from_line(1, 2)
-    from_ring(1, 1)
+    for s in (1, 2, 3):
+        zz = zplace(s)
+        arrived(kb.at[zz, c], k_recv.at[zz])
+        send(kb.at[zz, c], k_send.at[3 + s], k_sib.at[zz], sib)
+    for yy in (y_up, y_dn, y_far):
+        arrived(tb.at[yy], t_recv.at[yy])
     for s in range(4):
-        from_far(0, s)
-    from_line(1, 3)
-    from_sib(0)
-    permute(0, 0)
-    from_ring(1, 2)
-    permute(0, 1)
-    from_ring(1, 3)
-    permute(1, 0)
-    from_far(1, 0)
-    from_far(1, 1)
-    from_far(1, 2)
-    permute(1, 1)
-    from_far(1, 3)
+        zz = zplace(s)
+        arrived(kb.at[zz, 1 - c], k_sib.at[zz])
+
+    block = lax.dot_general(
+        tb[...].reshape(128, 1024), kb[...].reshape(256, 1024), NT, preferred_element_type=F32
+    ).astype(BF16)
+    gb[y, :, z, c] = block.reshape(4, 32, 256)
+
+    def part(yy, zz, cc):
+        return gb.at[yy, :, zz, cc]
+
+    for s in (1, 2, 3):
+        send(part(y, z, c), b_send.at[s], b_recv.at[y, z], at_train(y, zplace(s), c))
+    for i, d in enumerate(ring):
+        send(part(y, z, c), b_send.at[4 + i], b_recv.at[y, z], d)
+    send(part(y, z, c), b_send.at[0], b_sib.at[y, z], sib)
+    for s in (1, 2, 3):
+        zz = zplace(s)
+        arrived(part(y, zz, c), b_recv.at[y, zz])
+        for i, d in enumerate(ring):
+            send(part(y, zz, c), b_send.at[4 + 3 * s + i], b_recv.at[y, zz], d)
+        send(part(y, zz, c), b_send.at[15 + s], b_sib.at[y, zz], sib)
+    for s in range(4):
+        zz = zplace(s)
+        for i, yy in enumerate((y_up, y_dn, y_far)):
+            arrived(part(yy, zz, c), b_recv.at[yy, zz])
+            send(part(yy, zz, c), b_send.at[19 + 3 * s + i], b_sib.at[yy, zz], sib)
+
+    def blocks(h, p):
+        side = zh if h == 1 else 1 - zh
+        first, second = ((x + 2) % 4, x) if p == 0 else ((x + 1) % 4, (x + 3) % 4)
+        return (side * 4 + first) * 128, (side * 4 + second) * 128
+
+    def permute(h, p, yy):
+        a, b = blocks(h, p)
+        order = order_ref[...]
+        j = lax.broadcasted_iota(jnp.int32, (128, 1), 0)
+        pick = jnp.concatenate(
+            [(order == j + a).astype(F32).astype(BF16), (order == j + b).astype(F32).astype(BF16)], axis=0
+        )
+        rows = gb[yy].reshape(1024, 256)
+        cols = pl.ds(pl.multiple_of(yy * 256, 256), 256)
+        ob[2 * h + p, :, cols] = jnp.dot(pick, rows, preferred_element_type=F32).astype(BF16)
+
+    def permute_all(h, p):
+        def step(yy, carry):
+            permute(h, p, yy)
+            return carry
+        lax.fori_loop(0, 4, step, 0)
+
     loads[2].wait()
-    from_sib(1)
+    for yy in (y, y_up, y_dn, y_far):
+        for s in range(4):
+            zz = zplace(s)
+            arrived(part(yy, zz, 1 - c), b_sib.at[yy, zz])
+        permute(0, 0, yy)
 
     def tile(r, k):
         rows = pl.ds(pl.multiple_of(r * ROWS, ROWS), ROWS)
@@ -281,29 +239,21 @@
                     zs[r] = v.astype(BF16)
                     z_copy(r).start()
                 else:
-                    own[h, r] = v
+                    z_copy(r).wait_recv()
+                    rows = pl.ds(pl.multiple_of(r * ROWS, ROWS), ROWS)
+                    out_ref[rows, :] = (v + zr[r].astype(F32)) * 0.125
             return carry
         lax.fori_loop(0, 4, step, 0)
 
-    transform(0, 0)
     far_blocks(0)
-    transform(0, 1)
+    permute_all(0, 1)
     near_blocks(0)
-    transform(1, 0)
+    permute_all(1, 0)
     far_blocks(1)
-    transform(1, 1)
+    permute_all(1, 1)
     add_up(0)
     near_blocks(1)
     add_up(1)
-
-    def finish(i, carry):
-        for half in (0, 1):
-            r = i + 4 * half
-            z_copy(r).wait_recv()
-            rows = pl.ds(pl.multiple_of(r * ROWS, ROWS), ROWS)
-            out_ref[rows, :] = (own[1, r] + zr[r].astype(F32)) * 0.125
-        return carry
-    lax.fori_loop(0, 4, finish, 0)
 
     for cp in started:
         cp.wait_send()
@@ -329,8 +279,9 @@
         out_specs=vmem,
         scratch_shapes=[
             pltpu.VMEM((2048, 1024), BF16),
-            pltpu.VMEM((2, 32, 32, 1024), BF16),
-            pltpu.VMEM((4, 256, 1024), BF16),
+            pltpu.VMEM((4, 32, 1024), BF16),
+            pltpu.VMEM((4, 2, 32, 1024), BF16),
+            pltpu.VMEM((4, 4, 4, 2, 32, 256), BF16),
             pltpu.VMEM((4, 256, 1024), BF16),
             pltpu.VMEM((8, ROWS, 128), F32),
             pltpu.VMEM((2, 8, ROWS, 128), BF16),
@@ -344,10 +295,14 @@
             pltpu.VMEM((8, ROWS, 128), BF16),
             pltpu.VMEM((8, ROWS, 128), BF16),
             dma((3,)),
-            dma((2, 16)),
-            dma((2, 4, 4)),
-            dma((2, 4, 4)),
-            dma((2, 4, 4)),
+            dma((3,)),
+            dma((4,)),
+            dma((7,)),
+            dma((4,)),
+            dma((4,)),
+            dma((31,)),
+            dma((4, 4)),
+            dma((4, 4)),
             dma((2, 8)),
             dma((2, 8)),
             dma((2, 8)),

time: 87.4 us -> 79.1 us (0.905)
  the two profiles are of different devices: /device:TPU:1 before, /device:TPU:32 now
where the time goes in v2:
time: 79.1 us; the launch traced here: 79 us
  Pallas kernels  76.7 us (97%)
  local copies, waits for them, and re-layouts  2.26 us (3%)
    pallas_call x1, Pallas kernels, shards(): pl.pallas_call(kernel, out_shape=jax.ShapeDtypeStruct((2048, 128), F32),...  76.7 us
    unnamed x1, local copies, waits for them, and re-layouts  2.26 us

profile of v2, /device:TPU:32, one launch (start us, length us, event | category | flops | bytes accessed | tf_op | source)
XLA Modules:
  0.0 79.0 jit_solution(7633226992429651408)
XLA Ops:
  0.0 76.7 %scores.1 = f32[2048,128]{1,0:T(8,128)} custom-call(bf16[2048,1024]{1,0:T(8,128)(2,1)} %bitcast.5, bf16[32,1024]{1,0:T(8,128)(2,1)} %bitcast.6, bf16[32,1024]{1,0:T(8,128)(2,1)} %bitcast.7, f32[1,16]{1,0:T(1,128)} %bw_ref.1, s32[1,2048]{1,0:T(1,128)} %bitcast.8, s32[1,1024]{1,0:T(1,128)} %bitcast.9), custom_call_target="tpu_custom_call" | custom-call | tf_op jit(solution)/shard_map/scores/pallas_call | solution.py:275
  76.7 2.3 %copy.8 = f32[2048,128]{1,0:T(8,128)} copy(f32[2048,128]{1,0:T(8,128)} %scores.1) | data formatting | bytes 2097152

commit v3 on v2

--- a/solution.py
+++ b/solution.py
@@ -16,10 +16,10 @@
 
 
 def kernel(
-    train_hbm, test_hbm, kinv_hbm, bw_ref, bucket_ref, order_ref, out_ref,
-    train, tb, kb, gb, ob, wcol, s2, sp, sm, far_l, far_r, got_l, got_r, own, zs, zr,
-    load_sem, t_send, t_recv, k_send, k_recv, k_sib, b_send, b_recv, b_sib, s2_send, sp_send, sm_send,
-    far_l_recv, far_r_recv, got_l_recv, got_r_recv, z_send, z_recv,
+    train_hbm, test_hbm, kinv_hbm, bw_hbm, bucket_hbm, order_hbm, out_ref,
+    bw_ref, bucket_ref, order_ref, train, tb, kb, gb, ob, wcol, s2, sp, sm, far_l, far_r, got_l, got_r, own, zs, zr, zf,
+    ready, out_sem, load_sem, t_send, t_recv, k_send, k_recv, k_sib, b_send, b_recv, b_sib, s2_send, sp_send, sm_send,
+    far_l_recv, far_r_recv, got_l_recv, got_r_recv, z_send, z_recv, zf_recv,
 ):
     ck = lax.axis_index("ckpt")
     tr = lax.axis_index("train")
@@ -47,20 +47,30 @@
     right, left = at_ckpt(zh, (x + 1) % 4), at_ckpt(zh, (x + 3) % 4)
     across = at_ckpt(1 - zh, x)
 
+    barrier = pltpu.get_barrier_semaphore()
+    partners = [at_train(y, zplace(s), c) for s in (1, 2, 3)]
+    partners += [up, dn, at_train(y_far, z, c), right, left, sib]
+    for d in partners:
+        pl.semaphore_signal(barrier, inc=1, device_id=d, device_id_type=MESH)
+
+    @pl.when(zh == 0)
+    def _():
+        pl.semaphore_signal(barrier, inc=1, device_id=across, device_id_type=MESH)
+
     loads = [
-        pltpu.make_async_copy(test_hbm, tb.at[y], load_sem.at[0]),
-        pltpu.make_async_copy(kinv_hbm, kb.at[z, c], load_sem.at[1]),
-        pltpu.make_async_copy(train_hbm, train, load_sem.at[2]),
+        pltpu.make_async_copy(src, dst, load_sem.at[i])
+        for i, (src, dst) in enumerate((
+            (kinv_hbm, kb.at[z, c]), (test_hbm, tb.at[y]), (bw_hbm, bw_ref),
+            (bucket_hbm, bucket_ref), (order_hbm, order_ref), (train_hbm, train),
+        ))
     ]
     for cp in loads:
         cp.start()
-
-    barrier = pltpu.get_barrier_semaphore()
-    partners = [up, dn, at_train(y_far, z, c), sib, right, left, across]
-    partners += [at_train(y, zplace(s), c) for s in (1, 2, 3)]
-    for d in partners:
-        pl.semaphore_signal(barrier, inc=1, device_id=d, device_id_type=MESH)
-    pl.semaphore_wait(barrier, len(partners))
+    pl.semaphore_wait(barrier, len(partners) + zh)
+
+    @pl.when(zh == 1)
+    def _():
+        pl.semaphore_signal(ready, inc=1, device_id=across, device_id_type=MESH)
 
     started = []
 
@@ -78,13 +88,16 @@
 
     ring = [at_train(y_far, z, c), up, dn]
 
-    loads[1].wait()
+    loads[0].wait()
     for s in (1, 2, 3):
         send(kb.at[z, c], k_send.at[s], k_recv.at[z], at_train(y, zplace(s), c))
     send(kb.at[z, c], k_send.at[0], k_sib.at[z], sib)
-    loads[0].wait()
+    loads[1].wait()
     for i, d in enumerate(ring):
         send(tb.at[y], t_send.at[i], t_recv.at[y], d)
+
+    for i in (2, 3, 4):
+        loads[i].wait()
 
     eye = lax.broadcasted_iota(jnp.int32, (16, 16), 0) == lax.broadcasted_iota(jnp.int32, (16, 16), 1)
     col = jnp.sum(jnp.where(eye, jnp.broadcast_to(bw_ref[...], (16, 16)), 0.0), axis=1, keepdims=True)
@@ -162,7 +175,7 @@
             return carry
         lax.fori_loop(0, 4, step, 0)
 
-    loads[2].wait()
+    loads[5].wait()
     for yy in (y, y_up, y_dn, y_far):
         for s in range(4):
             zz = zplace(s)
@@ -197,6 +210,16 @@
         return pltpu.make_async_remote_copy(
             src_ref=zs.at[r], dst_ref=zr.at[r], send_sem=z_send.at[r],
             recv_sem=z_recv.at[r], device_id=across, device_id_type=MESH,
+        )
+
+    def out_copy(r):
+        rows = pl.ds(pl.multiple_of(r * ROWS, ROWS), ROWS)
+        return pltpu.make_async_copy(own.at[1, r], out_ref.at[rows, :], out_sem.at[r])
+
+    def early_copy(half):
+        return pltpu.make_async_remote_copy(
+            src_ref=s2.at[0, 3 + 4 * half], dst_ref=zf.at[half], send_sem=s2_send.at[0, 3 + 4 * half],
+            recv_sem=zf_recv.at[half], device_id=across, device_id_type=MESH,
         )
 
     def far_blocks(h):
@@ -208,27 +231,49 @@
                 own[h, r] = b
                 far_copy(h, i, r, half == 0).start()
             return carry
-        lax.fori_loop(0, 4, step, 0)
+        lax.fori_loop(0, 3, step, 0)
+
+    def far_last(h):
+        for half in (0, 1):
+            r = 3 + 4 * half
+            a, b = tile(r, 2 * h)
+            own[h, r] = b
+            if h == 0:
+                s2[h, r] = a.astype(BF16)
+                early_copy(half).start()
+            else:
+                early_copy(half).wait_recv()
+                s2[h, r] = (a + zf[half].astype(F32)).astype(BF16)
+                far_copy(h, 3, r, half == 0).start()
+
+    def near_block(h, i, add):
+        p, m = tile(i, 2 * h + 1)
+        sm[h, i] = m.astype(BF16)
+        left_copy(h, i).start()
+        if add:
+            far_copy(h, i, i, True).wait_recv()
+            p += far_l[h, i].astype(F32)
+        sp[h, i] = p.astype(BF16)
+        right_copy(h, i).start()
+        r = i + 4
+        p, m = tile(r, 2 * h + 1)
+        sp[h, r] = p.astype(BF16)
+        right_copy(h, r).start()
+        if add:
+            far_copy(h, i, r, False).wait_recv()
+            m += far_r[h, i].astype(F32)
+        sm[h, r] = m.astype(BF16)
+        left_copy(h, r).start()
 
     def near_blocks(h):
         def step(i, carry):
-            p, m = tile(i, 2 * h + 1)
-            sm[h, i] = m.astype(BF16)
-            left_copy(h, i).start()
-            far_copy(h, i, i, True).wait_recv()
-            sp[h, i] = (p + far_l[h, i].astype(F32)).astype(BF16)
-            right_copy(h, i).start()
-            r = i + 4
-            p, m = tile(r, 2 * h + 1)
-            sp[h, r] = p.astype(BF16)
-            right_copy(h, r).start()
-            far_copy(h, i, r, False).wait_recv()
-            sm[h, r] = (m + far_r[h, i].astype(F32)).astype(BF16)
-            left_copy(h, r).start()
+            near_block(h, i, True)
             return carry
-        lax.fori_loop(0, 4, step, 0)
-
-    def add_up(h):
+        lax.fori_loop(0, 3 if h == 0 else 4, step, 0)
+        if h == 0:
+            near_block(h, 3, False)
+
+    def add_up(h, first, last):
         def step(i, carry):
             for half in (0, 1):
                 r = i + 4 * half
@@ -240,20 +285,28 @@
                     z_copy(r).start()
                 else:
                     z_copy(r).wait_recv()
-                    rows = pl.ds(pl.multiple_of(r * ROWS, ROWS), ROWS)
-                    out_ref[rows, :] = (v + zr[r].astype(F32)) * 0.125
+                    own[1, r] = (v + zr[r].astype(F32)) * 0.125
+                    out_copy(r).start()
             return carry
-        lax.fori_loop(0, 4, step, 0)
+        lax.fori_loop(first, last, step, 0)
+
+    @pl.when(zh == 0)
+    def _():
+        pl.semaphore_wait(ready, 1)
 
     far_blocks(0)
+    far_last(0)
     permute_all(0, 1)
     near_blocks(0)
     permute_all(1, 0)
     far_blocks(1)
+    add_up(0, 0, 1)
     permute_all(1, 1)
-    add_up(0)
+    add_up(0, 1, 2)
+    far_last(1)
+    add_up(0, 2, 4)
     near_blocks(1)
-    add_up(1)
+    add_up(1, 0, 4)
 
     for cp in started:
         cp.wait_send()
@@ -264,6 +317,7 @@
             right_copy(h, r).wait_send()
             left_copy(h, r).wait_send()
         z_copy(r).wait_send()
+        out_copy(r).wait()
         return carry
     lax.fori_loop(0, 8, drain, 0)
 
@@ -275,9 +329,12 @@
     return pl.pallas_call(
         kernel,
         out_shape=jax.ShapeDtypeStruct((2048, 128), F32),
-        in_specs=[anywhere, anywhere, anywhere, vmem, vmem, vmem],
-        out_specs=vmem,
+        in_specs=[anywhere] * 6,
+        out_specs=pl.BlockSpec(memory_space=pl.ANY),
         scratch_shapes=[
+            pltpu.VMEM((1, 16), F32),
+            pltpu.VMEM((1, 2048), jnp.int32),
+            pltpu.VMEM((1, 1024), jnp.int32),
             pltpu.VMEM((2048, 1024), BF16),
             pltpu.VMEM((4, 32, 1024), BF16),
             pltpu.VMEM((4, 2, 32, 1024), BF16),
@@ -294,7 +351,10 @@
             pltpu.VMEM((2, 8, ROWS, 128), F32),
             pltpu.VMEM((8, ROWS, 128), BF16),
             pltpu.VMEM((8, ROWS, 128), BF16),
-            dma((3,)),
+            pltpu.VMEM((2, ROWS, 128), BF16),
+            pltpu.SemaphoreType.REGULAR,
+            dma((8,)),
+            dma((6,)),
             dma((3,)),
             dma((4,)),
             dma((7,)),
@@ -312,6 +372,7 @@
             dma((2, 8)),
             dma((8,)),
             dma((8,)),
+            dma((2,)),
         ],
         compiler_params=pltpu.CompilerParams(
             collective_id=0, has_side_effects=True, vmem_limit_bytes=60 * 1024 * 1024

time: 79.1 us -> 75.9 us (0.960)
  Pallas kernels: 76.7 us -> 73.5 us
    pallas_call x1, Pallas kernels: 76.7 us -> 73.5 us  [shards(): pl.pallas_call(kernel, out_shape=jax.ShapeDtypeStruct((2048, 128), F32),...]
where the time goes in v3:
time: 75.9 us; the launch traced here: 75.7 us
  Pallas kernels  73.5 us (97%)
  local copies, waits for them, and re-layouts  2.26 us (3%)
    pallas_call x1, Pallas kernels, shards(): pl.pallas_call(kernel, out_shape=jax.ShapeDtypeStruct((2048, 128), F32),...  73.5 us
    unnamed x1, local copies, waits for them, and re-layouts  2.26 us

profile of v3, /device:TPU:32, one launch (start us, length us, event | category | flops | bytes accessed | tf_op | source)
XLA Modules:
  0.0 75.7 jit_solution(14729765469816572379)
XLA Ops:
  0.0 73.5 %scores.1 = f32[2048,128]{1,0:T(8,128)} custom-call(bf16[2048,1024]{1,0:T(8,128)(2,1)} %bitcast.5, bf16[32,1024]{1,0:T(8,128)(2,1)} %bitcast.6, bf16[32,1024]{1,0:T(8,128)(2,1)} %bitcast.7, f32[1,16]{1,0:T(1,128)} %bw_hbm.1, s32[1,2048]{1,0:T(1,128)} %bitcast.8, s32[1,1024]{1,0:T(1,128)} %bitcast.9), custom_call_target="tpu_custom_call" | custom-call | tf_op jit(solution)/shard_map/scores/pallas_call | solution.py:329
  73.5 2.3 %copy.8 = f32[2048,128]{1,0:T(8,128)} copy(f32[2048,128]{1,0:T(8,128)} %scores.1) | data formatting | bytes 2097152

commit v4 on v3

--- a/solution.py
+++ b/solution.py
@@ -18,7 +18,7 @@
 def kernel(
     train_hbm, test_hbm, kinv_hbm, bw_hbm, bucket_hbm, order_hbm, out_ref,
     bw_ref, bucket_ref, order_ref, train, tb, kb, gb, ob, wcol, s2, sp, sm, far_l, far_r, got_l, got_r, own, zs, zr, zf,
-    ready, out_sem, load_sem, t_send, t_recv, k_send, k_recv, k_sib, b_send, b_recv, b_sib, s2_send, sp_send, sm_send,
+    ready, out_sem, load_sem, t_send, t_recv, k_send, k_recv, k_sib, b_send, b_recv, b_sib, l_send, l_recv, s2_send, sp_send, sm_send,
     far_l_recv, far_r_recv, got_l_recv, got_r_recv, z_send, z_recv, zf_recv,
 ):
     ck = lax.axis_index("ckpt")
@@ -141,16 +141,32 @@
     for i, d in enumerate(ring):
         send(part(y, z, c), b_send.at[4 + i], b_recv.at[y, z], d)
     send(part(y, z, c), b_send.at[0], b_sib.at[y, z], sib)
-    for s in (1, 2, 3):
+    def most(yy, zz):
+        return gb.at[yy, pl.ds(0, 3), zz, c]
+
+    def last(yy, zz):
+        return gb.at[yy, 3, zz, c]
+
+    def from_line(s):
         zz = zplace(s)
         arrived(part(y, zz, c), b_recv.at[y, zz])
         for i, d in enumerate(ring):
-            send(part(y, zz, c), b_send.at[4 + 3 * s + i], b_recv.at[y, zz], d)
+            send(most(y, zz), b_send.at[4 + 3 * s + i], b_recv.at[y, zz], d)
         send(part(y, zz, c), b_send.at[15 + s], b_sib.at[y, zz], sib)
-    for s in range(4):
+
+    from_line(1)
+    from_line(2)
+    for i, yy in enumerate((y_up, y_dn, y_far)):
+        arrived(part(yy, z, c), b_recv.at[yy, z])
+        for s in (1, 2, 3):
+            send(last(yy, z), l_send.at[3 * i + s - 1], l_recv.at[yy, z], at_train(y, zplace(s), c))
+        send(part(yy, z, c), b_send.at[19 + i], b_sib.at[yy, z], sib)
+    from_line(3)
+    for s in (1, 2, 3):
         zz = zplace(s)
         for i, yy in enumerate((y_up, y_dn, y_far)):
-            arrived(part(yy, zz, c), b_recv.at[yy, zz])
+            arrived(most(yy, zz), b_recv.at[yy, zz])
+            arrived(last(yy, zz), l_recv.at[yy, zz])
             send(part(yy, zz, c), b_send.at[19 + 3 * s + i], b_sib.at[yy, zz], sib)
 
     def blocks(h, p):
@@ -222,7 +238,7 @@
             recv_sem=zf_recv.at[half], device_id=across, device_id_type=MESH,
         )
 
-    def far_blocks(h):
+    def far_blocks(h, first, last):
         def step(i, carry):
             for half in (0, 1):
                 r = i + 4 * half
@@ -231,7 +247,7 @@
                 own[h, r] = b
                 far_copy(h, i, r, half == 0).start()
             return carry
-        lax.fori_loop(0, 3, step, 0)
+        lax.fori_loop(first, last, step, 0)
 
     def far_last(h):
         for half in (0, 1):
@@ -265,13 +281,11 @@
         sm[h, r] = m.astype(BF16)
         left_copy(h, r).start()
 
-    def near_blocks(h):
+    def near_blocks(h, first, last):
         def step(i, carry):
             near_block(h, i, True)
             return carry
-        lax.fori_loop(0, 3 if h == 0 else 4, step, 0)
-        if h == 0:
-            near_block(h, 3, False)
+        lax.fori_loop(first, last, step, 0)
 
     def add_up(h, first, last):
         def step(i, carry):
@@ -294,18 +308,23 @@
     def _():
         pl.semaphore_wait(ready, 1)
 
-    far_blocks(0)
+    far_blocks(0, 0, 1)
     far_last(0)
+    far_blocks(0, 1, 2)
     permute_all(0, 1)
-    near_blocks(0)
+    near_block(0, 3, False)
+    far_blocks(0, 2, 3)
+    near_blocks(0, 0, 2)
     permute_all(1, 0)
-    far_blocks(1)
+    add_up(0, 3, 4)
+    near_blocks(0, 2, 3)
+    far_blocks(1, 0, 3)
     add_up(0, 0, 1)
     permute_all(1, 1)
     add_up(0, 1, 2)
     far_last(1)
-    add_up(0, 2, 4)
-    near_blocks(1)
+    add_up(0, 2, 3)
+    near_blocks(1, 0, 4)
     add_up(1, 0, 4)
 
     for cp in started:
@@ -363,6 +382,8 @@
             dma((31,)),
             dma((4, 4)),
             dma((4, 4)),
+            dma((9,)),
+            dma((4, 4)),
             dma((2, 8)),
             dma((2, 8)),
             dma((2, 8)),

time: 75.9 us -> 71.8 us (0.946)
  the two profiles are of different devices: /device:TPU:32 before, /device:TPU:1 now
where the time goes in v4:
time: 71.8 us; the launch traced here: 71.7 us
  Pallas kernels  69.4 us (97%)
  local copies, waits for them, and re-layouts  2.26 us (3%)
    pallas_call x1, Pallas kernels, shards(): pl.pallas_call(kernel, out_shape=jax.ShapeDtypeStruct((2048, 128), F32),...  69.4 us
    unnamed x1, local copies, waits for them, and re-layouts  2.26 us

profile of v4, /device:TPU:1, one launch (start us, length us, event | category | flops | bytes accessed | tf_op | source)
XLA Modules:
  0.0 71.7 jit_solution(6808064897231227176)
XLA Ops:
  0.0 69.4 %scores.1 = f32[2048,128]{1,0:T(8,128)} custom-call(bf16[2048,1024]{1,0:T(8,128)(2,1)} %bitcast.5, bf16[32,1024]{1,0:T(8,128)(2,1)} %bitcast.6, bf16[32,1024]{1,0:T(8,128)(2,1)} %bitcast.7, f32[1,16]{1,0:T(1,128)} %bw_hbm.1, s32[1,2048]{1,0:T(1,128)} %bitcast.8, s32[1,1024]{1,0:T(1,128)} %bitcast.9), custom_call_target="tpu_custom_call" | custom-call | tf_op jit(solution)/shard_map/scores/pallas_call | solution.py:348
  69.4 2.3 %copy.8 = f32[2048,128]{1,0:T(8,128)} copy(f32[2048,128]{1,0:T(8,128)} %scores.1) | data formatting | bytes 2097152

commit v5 on v4

--- a/solution.py
+++ b/solution.py
@@ -17,7 +17,7 @@
 
 def kernel(
     train_hbm, test_hbm, kinv_hbm, bw_hbm, bucket_hbm, order_hbm, out_ref,
-    bw_ref, bucket_ref, order_ref, train, tb, kb, gb, ob, wcol, s2, sp, sm, far_l, far_r, got_l, got_r, own, zs, zr, zf,
+    bw_ref, bucket_ref, order_ref, by_place, train, tb, kb, gb, ob, wcol, s2, sp, sm, far_l, far_r, got_l, got_r, own, zs, zr, zf,
     ready, out_sem, load_sem, t_send, t_recv, k_send, k_recv, k_sib, b_send, b_recv, b_sib, l_send, l_recv, s2_send, sp_send, sm_send,
     far_l_recv, far_r_recv, got_l_recv, got_r_recv, z_send, z_recv, zf_recv,
 ):
@@ -98,6 +98,11 @@
 
     for i in (2, 3, 4):
         loads[i].wait()
+
+    order = order_ref[...]
+    by_place[...] = jnp.concatenate(
+        [order[:, 256 * i + 64 * k:256 * i + 64 * k + 64] for k in range(4) for i in range(4)], axis=1
+    )
 
     eye = lax.broadcasted_iota(jnp.int32, (16, 16), 0) == lax.broadcasted_iota(jnp.int32, (16, 16), 1)
     col = jnp.sum(jnp.where(eye, jnp.broadcast_to(bw_ref[...], (16, 16)), 0.0), axis=1, keepdims=True)
@@ -191,12 +196,25 @@
             return carry
         lax.fori_loop(0, 4, step, 0)
 
+    first_a, first_b = blocks(0, 0)
+    j = lax.broadcasted_iota(jnp.int32, (128, 1), 0)
+
+    def permute_from(zz, fresh):
+        order = by_place[:, pl.ds(pl.multiple_of(zz * 256, 256), 256)]
+        pick = jnp.concatenate(
+            [(order == j + first_a).astype(F32).astype(BF16), (order == j + first_b).astype(F32).astype(BF16)], axis=0
+        )
+        for yy in range(4):
+            cols = pl.ds(yy * 256, 256)
+            got = jnp.dot(pick, gb[yy, :, zz].reshape(256, 256), preferred_element_type=F32).astype(BF16)
+            ob[0, :, cols] = got if fresh else ob[0, :, cols] + got
+
     loads[5].wait()
-    for yy in (y, y_up, y_dn, y_far):
-        for s in range(4):
-            zz = zplace(s)
+    for s in range(4):
+        zz = zplace(s)
+        for yy in (y, y_up, y_dn, y_far):
             arrived(part(yy, zz, 1 - c), b_sib.at[yy, zz])
-        permute(0, 0, yy)
+        permute_from(zz, s == 0)
 
     def tile(r, k):
         rows = pl.ds(pl.multiple_of(r * ROWS, ROWS), ROWS)
@@ -353,6 +371,7 @@
         scratch_shapes=[
             pltpu.VMEM((1, 16), F32),
             pltpu.VMEM((1, 2048), jnp.int32),
+            pltpu.VMEM((1, 1024), jnp.int32),
             pltpu.VMEM((1, 1024), jnp.int32),
             pltpu.VMEM((2048, 1024), BF16),
             pltpu.VMEM((4, 32, 1024), BF16),

time: 71.8 us -> 70.9 us (0.987)
  Pallas kernels: 69.4 us -> 68.6 us
    pallas_call x1, Pallas kernels: 69.4 us -> 68.6 us  [shards(): pl.pallas_call(kernel, out_shape=jax.ShapeDtypeStruct((2048, 128), F32),...]
where the time goes in v5:
time: 70.9 us; the launch traced here: 70.8 us
  Pallas kernels  68.6 us (97%)
  local copies, waits for them, and re-layouts  2.26 us (3%)
    pallas_call x1, Pallas kernels, shards(): pl.pallas_call(kernel, out_shape=jax.ShapeDtypeStruct((2048, 128), F32),...  68.6 us
    unnamed x1, local copies, waits for them, and re-layouts  2.26 us

profile of v5, /device:TPU:1, one launch (start us, length us, event | category | flops | bytes accessed | tf_op | source)
XLA Modules:
  0.0 70.8 jit_solution(10888306557908892836)
XLA Ops:
  0.0 68.6 %scores.1 = f32[2048,128]{1,0:T(8,128)} custom-call(bf16[2048,1024]{1,0:T(8,128)(2,1)} %bitcast.5, bf16[32,1024]{1,0:T(8,128)(2,1)} %bitcast.6, bf16[32,1024]{1,0:T(8,128)(2,1)} %bitcast.7, f32[1,16]{1,0:T(1,128)} %bw_hbm.1, s32[1,2048]{1,0:T(1,128)} %bitcast.8, s32[1,1024]{1,0:T(1,128)} %bitcast.9), custom_call_target="tpu_custom_call" | custom-call | tf_op jit(solution)/shard_map/scores/pallas_call | solution.py:366
  68.6 2.3 %copy.8 = f32[2048,128]{1,0:T(8,128)} copy(f32[2048,128]{1,0:T(8,128)} %scores.1) | data formatting | bytes 2097152

commit v6 on v5

--- a/solution.py
+++ b/solution.py
@@ -86,7 +86,7 @@
             src_ref=ref, dst_ref=ref, send_sem=b_send.at[0], recv_sem=recv_sem, device_id=sib, device_id_type=MESH,
         ).wait_recv()
 
-    ring = [at_train(y_far, z, c), up, dn]
+    ring = [up, dn, at_train(y_far, z, c)]
 
     loads[0].wait()
     for s in (1, 2, 3):

time: 70.9 us -> 70.7 us (level)
  no operation moved by 1% of the time
where the time goes in v6:
time: 70.7 us; the launch traced here: 70.5 us
  Pallas kernels  68.3 us (97%)
  local copies, waits for them, and re-layouts  2.26 us (3%)
    pallas_call x1, Pallas kernels, shards(): pl.pallas_call(kernel, out_shape=jax.ShapeDtypeStruct((2048, 128), F32),...  68.3 us
    unnamed x1, local copies, waits for them, and re-layouts  2.26 us

profile of v6, /device:TPU:1, one launch (start us, length us, event | category | flops | bytes accessed | tf_op | source)
XLA Modules:
  0.0 70.5 jit_solution(6357391525384273915)
XLA Ops:
  0.0 68.3 %scores.1 = f32[2048,128]{1,0:T(8,128)} custom-call(bf16[2048,1024]{1,0:T(8,128)(2,1)} %bitcast.5, bf16[32,1024]{1,0:T(8,128)(2,1)} %bitcast.6, bf16[32,1024]{1,0:T(8,128)(2,1)} %bitcast.7, f32[1,16]{1,0:T(1,128)} %bw_hbm.1, s32[1,2048]{1,0:T(1,128)} %bitcast.8, s32[1,1024]{1,0:T(1,128)} %bitcast.9), custom_call_target="tpu_custom_call" | custom-call | tf_op jit(solution)/shard_map/scores/pallas_call | solution.py:366
  68.3 2.3 %copy.8 = f32[2048,128]{1,0:T(8,128)} copy(f32[2048,128]{1,0:T(8,128)} %scores.1) | data formatting | bytes 2097152
